TPU v7x, 32 devices: a whole 2x2x4 slice. The times are simulated.
32 devices in a mesh: dp: 8 (over z, x), fsdp: 4 (over y, core).
Axes of the slice: x: 2, y: 2, z: 4, core: 2. Of those that a mesh axis runs over, the one named last changes fastest.
Arguments:
- tokens: bfloat16 [64, 512, 768], P(('dp', 'fsdp')), may hold values from -6 to 6
- segments: int32 [64, 512], P(('dp', 'fsdp')), may hold values from 0 to 11, never falling along the last dimension, each value on 1 to 256 neighbouring positions
- w_query: bfloat16 [768, 768], P(('dp', 'fsdp')), may hold values from -0.21875 to 0.21875
- w_key: bfloat16 [768, 768], P(('dp', 'fsdp')), may hold values from -0.21875 to 0.21875
- w_value: bfloat16 [768, 768], P(('dp', 'fsdp')), may hold values from -0.21875 to 0.21875
- w_output: bfloat16 [768, 768], P(('dp', 'fsdp')), may hold values from -1.25 to 1.25
- w_inner: bfloat16 [768, 3072], P(('dp', 'fsdp')), may hold values from -0.21875 to 0.21875
- w_outer: bfloat16 [3072, 768], P(('dp', 'fsdp')), may hold values from -0.109375 to 0.109375
- down_query: bfloat16 [768, 8], P(('dp', 'fsdp')), may hold values from -0.21875 to 0.21875
- down_value: bfloat16 [768, 8], P(('dp', 'fsdp')), may hold values from -0.21875 to 0.21875
- up_query: bfloat16 [8, 768], replicated, may hold values from -0.59765625 to 0.59765625
- up_value: bfloat16 [8, 768], replicated, may hold values from -0.59765625 to 0.59765625
- norm1_gain: float32 [768], replicated, may hold values from 0.5 to 1.5
- norm1_shift: float32 [768], replicated, may hold values from -1.5 to 1.5
- norm2_gain: float32 [768], replicated, may hold values from 0.5 to 1.5
- norm2_shift: float32 [768], replicated, may hold values from -1.5 to 1.5
- out_grad: bfloat16 [64, 512, 768], P(('dp', 'fsdp')), may hold values from -6 to 6
Outputs:
- layer_out: bfloat16 [64, 512, 768], P(('dp', 'fsdp'))
- tokens_grad: bfloat16 [64, 512, 768], P(('dp', 'fsdp'))
- up_query_grad: float32 [8, 768], replicated
- up_value_grad: float32 [8, 768], replicated
Inputs may be any that keep to these rules, and one draw needn't show every extreme that they name: `segments`: within each packed row the segment numbers never fall; each item spans 1 to 256 positions, and some item spans exactly 256.
All inputs are finite; a program needn't handle non-finite values.
Results may differ from a plain program's by a relative error of at most 0.014.
The roundings to bfloat16 on the way count: a program that leaves them out, or rounds other values in their place, can miss the bound.
Values may be sent and summed in bfloat16 or wider, within the bound.
A program may use at most 128 MiB of HBM per device.

v0:
```python
import jax
import jax.numpy as jnp
from jax import lax
from jax.sharding import PartitionSpec as P

H = 12
HD = 64


def gelu_exact(values):
    return jax.nn.gelu(values, approximate=False)


def normalize(values):
    center = values - jnp.mean(values, axis=-1, keepdims=True)
    scaler = lax.rsqrt(jnp.mean(center * center, axis=-1, keepdims=True) + 1e-05)
    return (center * scaler, scaler)


def norm_back(grad_normed, normed, scaler):
    first = jnp.mean(grad_normed, axis=-1, keepdims=True)
    second = jnp.mean(grad_normed * normed, axis=-1, keepdims=True)
    return scaler * (grad_normed - first - normed * second)


def row_scores(q_row, k_row, seg_row):
    same = seg_row[:, None] == seg_row[None, :]
    scores = jnp.einsum("qhd,khd->hqk", q_row, k_row, preferred_element_type=jnp.float32) * 0.125
    return jnp.where(same[None], scores, -1e30)


def body(
    tokens,
    segments,
    w_query,
    w_key,
    w_value,
    w_output,
    w_inner,
    w_outer,
    down_query,
    down_value,
    up_query,
    up_value,
    norm1_gain,
    norm1_shift,
    norm2_gain,
    norm2_shift,
    out_grad,
):
    row_count, length, width = tokens.shape
    count = row_count * length
    whole = (
        lax.all_gather(w_query, ("dp", "fsdp"), axis=0, tiled=True),
        lax.all_gather(w_key, ("dp", "fsdp"), axis=0, tiled=True),
        lax.all_gather(w_value, ("dp", "fsdp"), axis=0, tiled=True),
        lax.all_gather(w_output, ("dp", "fsdp"), axis=0, tiled=True),
        lax.all_gather(w_inner, ("dp", "fsdp"), axis=0, tiled=True),
        lax.all_gather(w_outer, ("dp", "fsdp"), axis=0, tiled=True),
        lax.all_gather(down_query, ("dp", "fsdp"), axis=0, tiled=True),
        lax.all_gather(down_value, ("dp", "fsdp"), axis=0, tiled=True),
    )
    wq, wk, wv, wo, win, wout, dq_mat, dv_mat = whole
    tok_rows = tokens.reshape(count, width)
    low_q = jnp.dot(tok_rows, dq_mat, preferred_element_type=jnp.float32).astype(jnp.bfloat16)
    low_v = jnp.dot(tok_rows, dv_mat, preferred_element_type=jnp.float32).astype(jnp.bfloat16)
    queries = (
        jnp.dot(tok_rows, wq, preferred_element_type=jnp.float32)
        + 2.0 * jnp.dot(low_q, up_query, preferred_element_type=jnp.float32)
    ).astype(jnp.bfloat16)
    keys_all = jnp.dot(tok_rows, wk, preferred_element_type=jnp.float32).astype(jnp.bfloat16)
    values_all = (
        jnp.dot(tok_rows, wv, preferred_element_type=jnp.float32)
        + 2.0 * jnp.dot(low_v, up_value, preferred_element_type=jnp.float32)
    ).astype(jnp.bfloat16)
    q_heads = queries.reshape(row_count, length, H, HD)
    k_heads = keys_all.reshape(row_count, length, H, HD)
    v_heads = values_all.reshape(row_count, length, H, HD)

    def attend(items):
        q_row, k_row, v_row, seg_row = items
        masked = row_scores(q_row, k_row, seg_row)
        highest = jnp.max(masked, axis=-1, keepdims=True)
        expos = jnp.exp(masked - highest)
        totals = jnp.sum(expos, axis=-1, keepdims=True)
        probs = (expos / totals).astype(jnp.bfloat16)
        context = jnp.einsum("hqk,khd->qhd", probs, v_row, preferred_element_type=jnp.float32)
        return (context.astype(jnp.bfloat16), highest + jnp.log(totals))

    contexts, log_totals = lax.map(attend, (q_heads, k_heads, v_heads, segments))
    context_rows = contexts.reshape(count, width)
    summed1 = tok_rows.astype(jnp.float32) + jnp.dot(
        context_rows, wo, preferred_element_type=jnp.float32
    )
    normed1, scaler1 = normalize(summed1)
    hidden1 = normed1 * norm1_gain + norm1_shift
    hidden_low = hidden1.astype(jnp.bfloat16)
    inner = jnp.dot(hidden_low, win, preferred_element_type=jnp.float32)
    active = gelu_exact(inner).astype(jnp.bfloat16)
    summed2 = hidden1 + jnp.dot(active, wout, preferred_element_type=jnp.float32)
    normed2, scaler2 = normalize(summed2)
    layer_out = (normed2 * norm2_gain + norm2_shift).astype(jnp.bfloat16)
    second = (
        lax.all_gather(w_query, ("dp", "fsdp"), axis=0, tiled=True),
        lax.all_gather(w_key, ("dp", "fsdp"), axis=0, tiled=True),
        lax.all_gather(w_value, ("dp", "fsdp"), axis=0, tiled=True),
        lax.all_gather(w_output, ("dp", "fsdp"), axis=0, tiled=True),
        lax.all_gather(w_inner, ("dp", "fsdp"), axis=0, tiled=True),
        lax.all_gather(w_outer, ("dp", "fsdp"), axis=0, tiled=True),
        lax.all_gather(down_query, ("dp", "fsdp"), axis=0, tiled=True),
        lax.all_gather(down_value, ("dp", "fsdp"), axis=0, tiled=True),
    )
    wq, wk, wv, wo, win, wout, dq_mat, dv_mat = second
    cotangent = out_grad.reshape(count, width).astype(jnp.float32)
    grad_sum2 = norm_back(cotangent * norm2_gain, normed2, scaler2)
    grad_branch = grad_sum2.astype(jnp.bfloat16)
    inner_again = jnp.dot(hidden_low, win, preferred_element_type=jnp.float32)
    gelu_value, gelu_pull = jax.vjp(gelu_exact, inner_again)
    grad_active = jnp.dot(grad_branch, wout.T, preferred_element_type=jnp.float32)
    grad_inner = gelu_pull(grad_active)[0].astype(jnp.bfloat16)
    grad_hidden = grad_sum2 + jnp.dot(grad_inner, win.T, preferred_element_type=jnp.float32)
    grad_sum1 = norm_back(grad_hidden * norm1_gain, normed1, scaler1)
    grad_attended = grad_sum1.astype(jnp.bfloat16)
    grad_context = jnp.dot(grad_attended, wo.T, preferred_element_type=jnp.float32).astype(
        jnp.bfloat16
    )
    grad_heads = grad_context.reshape(row_count, length, H, HD)

    def attend_back(items):
        q_row, k_row, v_row, seg_row, lse_row, grad_row = items
        masked = row_scores(q_row, k_row, seg_row)
        probs = jnp.exp(masked - lse_row)
        grad_v = jnp.einsum(
            "hqk,qhd->khd", probs.astype(jnp.bfloat16), grad_row, preferred_element_type=jnp.float32
        )
        grad_probs = jnp.einsum("qhd,khd->hqk", grad_row, v_row, preferred_element_type=jnp.float32)
        inner_sum = jnp.sum(grad_probs * probs, axis=-1, keepdims=True)
        grad_scores = (probs * (grad_probs - inner_sum)).astype(jnp.bfloat16)
        grad_q = (
            jnp.einsum("hqk,khd->qhd", grad_scores, k_row, preferred_element_type=jnp.float32)
            * 0.125
        )
        grad_k = (
            jnp.einsum("hqk,qhd->khd", grad_scores, q_row, preferred_element_type=jnp.float32)
            * 0.125
        )
        return (
            grad_q.astype(jnp.bfloat16),
            grad_k.astype(jnp.bfloat16),
            grad_v.astype(jnp.bfloat16),
        )

    grad_qh, grad_kh, grad_vh = lax.map(
        attend_back, (q_heads, k_heads, v_heads, segments, log_totals, grad_heads)
    )
    grad_query = grad_qh.reshape(count, width)
    grad_key = grad_kh.reshape(count, width)
    grad_value = grad_vh.reshape(count, width)
    grad_low_q = (2.0 * jnp.dot(grad_query, up_query.T, preferred_element_type=jnp.float32)).astype(
        jnp.bfloat16
    )
    grad_low_v = (2.0 * jnp.dot(grad_value, up_value.T, preferred_element_type=jnp.float32)).astype(
        jnp.bfloat16
    )
    grad_tokens = grad_sum1 + jnp.dot(grad_query, wq.T, preferred_element_type=jnp.float32)
    grad_tokens = grad_tokens + jnp.dot(grad_key, wk.T, preferred_element_type=jnp.float32)
    grad_tokens = grad_tokens + jnp.dot(grad_value, wv.T, preferred_element_type=jnp.float32)
    grad_tokens = grad_tokens + jnp.dot(grad_low_q, dq_mat.T, preferred_element_type=jnp.float32)
    grad_tokens = grad_tokens + jnp.dot(grad_low_v, dv_mat.T, preferred_element_type=jnp.float32)
    local_q = 2.0 * jnp.einsum("tr,td->rd", low_q, grad_query, preferred_element_type=jnp.float32)
    local_v = 2.0 * jnp.einsum("tr,td->rd", low_v, grad_value, preferred_element_type=jnp.float32)
    total_q, total_v = lax.psum((local_q, local_v), ("dp", "fsdp"))
    return (
        layer_out.reshape(row_count, length, width),
        grad_tokens.astype(jnp.bfloat16).reshape(row_count, length, width),
        total_q,
        total_v,
    )


def solution(mesh):
    placed = (
        P(("dp", "fsdp"), None, None),
        P(("dp", "fsdp"), None),
        P(("dp", "fsdp"), None),
        P(("dp", "fsdp"), None),
        P(("dp", "fsdp"), None),
        P(("dp", "fsdp"), None),
        P(("dp", "fsdp"), None),
        P(("dp", "fsdp"), None),
        P(("dp", "fsdp"), None),
        P(("dp", "fsdp"), None),
        P(),
        P(),
        P(),
        P(),
        P(),
        P(),
        P(("dp", "fsdp"), None, None),
    )
    return jax.shard_map(
        body,
        mesh=mesh,
        in_specs=placed,
        out_specs=(P(("dp", "fsdp"), None, None), P(("dp", "fsdp"), None, None), P(), P()),
        check_vma=False,
    )
```

profile of v0, /device:TPU:0, one launch (start us, length us, event | category | flops | bytes accessed | tf_op | source)
XLA Modules:
  0.0 558.4 jit_solution(10017231867190146173)
XLA Ops:
  11.2 43.6 %all-gather = bf16[32,24,8]{1,2,0:T(8,128)(2,1)S(1)} all-gather(bf16[1,24,8]{1,2,0:T(8,128)(2,1)} %bitcast.217), channel_id=1, replica_groups=mesh['dp'=8,'fsdp'=4] {'dp','fsdp'}, dimensions={0}, use_global_device_ids=true | all-gather | bytes 12672 | tf_op jit(solution)/shard_map/all_gather | solution.py:61
  55.0 37.1 %all-gather.1 = bf16[32,24,8]{1,2,0:T(8,128)(2,1)S(1)} all-gather(bf16[1,24,8]{1,2,0:T(8,128)(2,1)} %bitcast.218), channel_id=1, replica_groups=mesh['dp'=8,'fsdp'=4] {'dp','fsdp'}, dimensions={0}, use_global_device_ids=true | all-gather | bytes 12672 | tf_op jit(solution)/shard_map/all_gather | solution.py:60
  108.5 15.2 %all-gather.11.cloned.1.call-done = bf16[768,768]{1,0:T(8,128)(2,1)} async-done(((bf16[24,768]{1,0:T(8,128)(2,1)}), bf16[768,768]{1,0:T(8,128)(2,1)}) %all-gather.11.cloned.1.call-update) | async-done | bytes 1179664 | tf_op jit(solution)/shard_map/all_gather | solution.py:54
  134.0 45.7 %all-gather.13.cloned.1.call-done = bf16[768,768]{1,0:T(8,128)(2,1)} async-done(((bf16[24,768]{1,0:T(8,128)(2,1)}), bf16[768,768]{1,0:T(8,128)(2,1)}) %all-gather.13.cloned.1.call-update) | async-done | bytes 1179664 | tf_op jit(solution)/shard_map/all_gather | solution.py:55
  190.7 20.9 %while.26 = (s32[]{:T(128)}, bf16[2,512,12,64]{1,3,2,0:T(8,128)(2,1)}, f32[2,12,512,1]{2,1,3,0:T(8,128)S(1)}, bf16[2,512,12,64]{1,3,2,0:T(8,128)(2,1)}, s32[2,51...) while((s32[]{:T(128)}, ...), condition=%wide.region_3.4_spmd, body=%wide.region_0.3_spmd.sunk | while | flops 843704320 | bytes 42172508 | solution.py:90
  195.8 5.4 fusion.162
  206.2 5.4 fusion.162
  216.2 19.4 %all-gather.15.cloned.1.call-done = bf16[768,768]{1,0:T(8,128)(2,1)} async-done(((bf16[24,768]{1,0:T(8,128)(2,1)}), bf16[768,768]{1,0:T(8,128)(2,1)}) %all-gather.15.cloned.1.call-update) | async-done | bytes 1179664 | tf_op jit(solution)/shard_map/all_gather | solution.py:57
  235.6 5.4 fusion.89
  243.4 57.5 %all-gather.17.cloned.1.call-done = bf16[768,3072]{1,0:T(8,128)(2,1)} async-done(((bf16[24,3072]{1,0:T(8,128)(2,1)}), bf16[768,3072]{1,0:T(8,128)(2,1)}) %all-gather.17.cloned.1.call-update) | async-done | bytes 4718608 | tf_op jit(solution)/shard_map/all_gather | solution.py:58
  300.9 36.5 %fusion.57 = (f32[1024,3072]{1,0:T(8,128)}, f32[1024,3072]{1,0:T(8,128)}) fusion(bf16[768,3072]{1,0:T(8,128)(2,1)} %all-gather.17.cloned.1.call-done, f32[1024,768]{1,0:T(8,128)} %get-tuple-element.197, f32[768]{0:T(1024)S(1)} %copy-done.39, f32[768]{0:T(1024)S(1)} %copy-done.40, f32[1024]{0:T(1024)S(1)} %add_rsqrt_fusion.1, ...), kind=kOutput, calls=%fused_computation.65 | convolution fusion | flops 5030805504 | bytes 33044480 | tf_op jit(solution)/shard_map/dot_general | solution.py:98
  337.4 28.7 %all-gather.19.cloned.1.call-done = bf16[3072,768]{1,0:T(8,128)(2,1)} async-done(((bf16[96,768]{1,0:T(8,128)(2,1)}), bf16[3072,768]{1,0:T(8,128)(2,1)}) %all-gather.19.cloned.1.call-update) | async-done | bytes 4718608 | tf_op jit(solution)/shard_map/all_gather | solution.py:59
  366.1 15.6 %fusion.90 = (f32[1024]{0:T(1024)S(1)}, f32[1024,768]{1,0:T(8,128)S(1)}) fusion(bf16[3072,768]{1,0:T(8,128)(2,1)} %all-gather.19.cloned.1.call-done, f32[1024,3072]{1,0:T(8,128)} %get-tuple-element.198, f32[1024,3072]{1,0:T(8,128)} %get-tuple-element.199, f32[768]{0:T(1024)S(1)} %copy-done.39, f32[768]{0:T(1024)S(1)} %copy-done.40, ...), kind=kOutput, calls=%fused_computation.140 | convolution fusion | flops 4845992960 | bytes 36194304 | tf_op jit(solution)/shard_map/dot_general | solution.py:100
  387.1 22.7 %fusion.88 = (f32[1024]{0:T(1024)S(1)}, f32[1024]{0:T(1024)S(1)}, f32[1024,768]{1,0:T(8,128)}) fusion(f32[1024]{0:T(1024)S(1)} %add_rsqrt_fusion.1, f32[1024,768]{1,0:T(8,128)} %get-tuple-element.197, f32[1024]{0:T(1024)S(1)} %broadcast_multiply_fusion.4, f32[768]{0:T(1024)S(1)} %copy-done.40, f32[1024,768]{1,0:T(8,128)} %get-tuple-element.194, ...), kind=kOutput, calls=%fused_computation.138 | convolution fusion | flops 9714006016 | bytes 44059648 | tf_op jit(solution)/shard_map/dot_general | solution.py:121
  409.9 6.1 %convolution_convert_fusion = bf16[1024,768]{1,0:T(8,128)(2,1)} fusion(bf16[768,768]{1,0:T(8,128)(2,1)} %all-gather.15.cloned.1.call-done, f32[1024,768]{1,0:T(8,128)} %get-tuple-element.202, f32[1024,768]{1,0:T(8,128)} %get-tuple-element.197, f32[1024]{0:T(1024)S(1)} %get-tuple-element.203, f32[1024]{0:T(1024)S(1)} %get-tuple-element.204, ...), kind=kOutput, calls=%fused_computation.103 | convolution fusion | flops 1214251008 | bytes 9060352 | tf_op jit(solution)/shard_map/dot_general | solution.py:124
  429.3 48.3 %while.27 = (s32[]{:T(128)}, bf16[2,512,12,64]{1,3,2,0:T(8,128)(2,1)}, bf16[2,512,12,64]{1,3,2,0:T(8,128)(2,1)}, bf16[2,512,12,64]{1,3,2,0:T(8,128)(2,1)}, bf16[...) while((s32[]{:T(128)}, ...), condition=%wide.region_14.15_spmd, body=%wide.region_12.14_spmd.sunk | while | flops 2062673920 | bytes 147524944 | solution.py:153
  431.4 6.7 %multiply_reduce_fusion.7 = (f32[12,512]{1,0:T(8,128)S(1)}, f32[12,512,512]{1,2,0:T(8,128)}) fusion(f32[12,512,512]{1,2,0:T(8,128)S(1)} %fusion.171, f32[12,512]{1,0:T(8,128)S(1)} %dynamic-slice_bitcast_fusion.2, pred[512,512]{0,1:T(8,128)(4,1)S(1)} %broadcast_compare_fusion.5, bf16[2,512,12,64]{1,3,2,0:T(8,128)(2,1)S(1)} %copy-done.1, ...), kind=kOutput, calls=%fused_computation.24.clone.1 | convolution fusion | flops 418375680 | bytes 27059200 | tf_op jit(solution)/shard_map/while/body/eval_jaxpr/qhd,khd->hqk/dot_general | solution.py:136
  438.2 6.8 %multiply_convert_fusion.8 = bf16[12,512,512]{1,2,0:T(8,128)(2,1)S(1)} fusion(f32[12,512,512]{1,2,0:T(8,128)} %get-tuple-element.315, f32[12,512,512]{1,2,0:T(8,128)S(1)} %fusion.171, f32[12,512]{1,0:T(8,128)S(1)} %get-tuple-element.316, f32[12,512]{1,0:T(8,128)S(1)} %dynamic-slice_bitcast_fusion.2, pred[512,512]{0,1:T(8,128)(4,1)S(1)} %broadcast_compare_fusion.5), kind=kLoop, calls=%fused_computation.23.clone.1 | loop fusion | flops 18874368 | bytes 31768576 | tf_op jit(solution)/shard_map/while/body/eval_jaxpr/convert_element_type | solution.py:138
  449.4 4.0 fusion.174
  455.5 6.7 %multiply_reduce_fusion.7 = (f32[12,512]{1,0:T(8,128)S(1)}, f32[12,512,512]{1,2,0:T(8,128)}) fusion(f32[12,512,512]{1,2,0:T(8,128)S(1)} %fusion.171, f32[12,512]{1,0:T(8,128)S(1)} %dynamic-slice_bitcast_fusion.2, pred[512,512]{0,1:T(8,128)(4,1)S(1)} %broadcast_compare_fusion.5, bf16[2,512,12,64]{1,3,2,0:T(8,128)(2,1)S(1)} %copy-done.1, ...), kind=kOutput, calls=%fused_computation.24.clone.1 | convolution fusion | flops 418375680 | bytes 27059200 | tf_op jit(solution)/shard_map/while/body/eval_jaxpr/qhd,khd->hqk/dot_general | solution.py:136
  462.2 6.8 %multiply_convert_fusion.8 = bf16[12,512,512]{1,2,0:T(8,128)(2,1)S(1)} fusion(f32[12,512,512]{1,2,0:T(8,128)} %get-tuple-element.315, f32[12,512,512]{1,2,0:T(8,128)S(1)} %fusion.171, f32[12,512]{1,0:T(8,128)S(1)} %get-tuple-element.316, f32[12,512]{1,0:T(8,128)S(1)} %dynamic-slice_bitcast_fusion.2, pred[512,512]{0,1:T(8,128)(4,1)S(1)} %broadcast_compare_fusion.5), kind=kLoop, calls=%fused_computation.23.clone.1 | loop fusion | flops 18874368 | bytes 31768576 | tf_op jit(solution)/shard_map/while/body/eval_jaxpr/convert_element_type | solution.py:138
  490.4 40.9 %all-reduce = (f32[8,768]{1,0:T(8,128)}, f32[8,768]{1,0:T(8,128)}) all-reduce(f32[8,768]{1,0:T(8,128)S(1)} %convolution_multiply_fusion.3, f32[8,768]{1,0:T(8,128)S(1)} %convolution_multiply_fusion.2), channel_id=1, replica_groups=mesh['dp'=8,'fsdp'=4] {'dp','fsdp'}, use_global_device_ids=true, to_apply=%region_15.16 | all-reduce | flops 12288 | bytes 98304 | tf_op jit(solution)/shard_map/psum | solution.py:172
  531.3 4.5 fusion.93
  542.3 8.9 %add_convert_fusion.2 = bf16[1024,768]{1,0:T(8,128)(2,1)} fusion(f32[1024,768]{1,0:T(8,128)} %fusion.79, f32[1024,768]{1,0:T(8,128)} %fusion.95, f32[1024,768]{1,0:T(8,128)} %fusion.94, f32[1024,768]{1,0:T(8,128)} %fusion.93, bf16[768,8]{0,1:T(8,128)(2,1)S(1)} %copy-done.19, bf16[1024,768]{0,1:T(8,128)(2,1)S(1)} %bitcast.196, ...), kind=kOutput, calls=%fused_computation.85 | convolution fusion | flops 34619392 | bytes 22061056 | tf_op jit(solution)/shard_map/dot_general | solution.py:169
  (186 shorter events, 113.1 us)
Async XLA Ops:
  7.2 119.3 %copy-start = (bf16[8,768]{1,0:T(8,128)(2,1)S(1)}, bf16[8,768]{1,0:T(8,128)(2,1)}, u32[]{:S(2)}) copy-start(bf16[8,768]{1,0:T(8,128)(2,1)} %param.31) | copy-start | bytes 36868
  7.2 89.9 %copy-start.6 = (bf16[2,512,768]{2,1,0:T(8,128)(2,1)S(1)}, bf16[2,512,768]{2,1,0:T(8,128)(2,1)}, u32[]{:S(2)}) copy-start(bf16[2,512,768]{2,1,0:T(8,128)(2,1)} %param.21) | copy-start | bytes 4718596
  7.2 88.9 %copy-start.25 = (f32[768]{0:T(1024)S(1)}, f32[768]{0:T(1024)}, u32[]{:S(2)}) copy-start(f32[768]{0:T(1024)} %param.35) | copy-start | bytes 9220
  7.2 88.9 %copy-start.4 = (bf16[2,512,768]{2,1,0:T(8,128)(2,1)S(1)}, bf16[2,512,768]{2,1,0:T(8,128)(2,1)}, u32[]{:S(2)}) copy-start(bf16[2,512,768]{2,1,0:T(8,128)(2,1)} %param.37) | copy-start | bytes 4718596
  7.2 89.9 %all-gather.9.cloned.1.call-start = ((), (), s32[]{:S(2)}) async-start(), calls=%async_computation | async-start | bytes 1216512 | tf_op jit(solution)/shard_map/all_gather | solution.py:56
  8.0 115.8 %all-gather.11.cloned.1.call-start = ((), (), s32[]{:S(2)}) async-start(), calls=%async_computation.1 | async-start | bytes 1216512 | tf_op jit(solution)/shard_map/all_gather | solution.py:54
  8.7 171.0 %all-gather.13.cloned.1.call-start = ((), (), s32[]{:S(2)}) async-start(), calls=%async_computation.2 | async-start | bytes 1216512 | tf_op jit(solution)/shard_map/all_gather | solution.py:55
  9.4 226.1 %all-gather.15.cloned.1.call-start = ((), (), s32[]{:S(2)}) async-start(), calls=%async_computation.3 | async-start | bytes 1216512 | tf_op jit(solution)/shard_map/all_gather | solution.py:57
  10.0 290.9 %all-gather.17.cloned.1.call-start = ((), (), s32[]{:S(2)}) async-start(), calls=%async_computation.4 | async-start | bytes 4866048 | tf_op jit(solution)/shard_map/all_gather | solution.py:58
  10.6 355.5 %all-gather.19.cloned.1.call-start = ((), (), s32[]{:S(2)}) async-start(), calls=%async_computation.5 | async-start | bytes 4866048 | tf_op jit(solution)/shard_map/all_gather | solution.py:59
  55.0 44.8 %copy-start.18 = (bf16[768,8]{0,1:T(8,128)(2,1)}, bf16[768,8]{0,1:T(8,128)(2,1)S(1)}, u32[]{:S(2)}) copy-start(bf16[768,8]{0,1:T(8,128)(2,1)S(1)} %reshape.197) | copy-start | bytes 36868
  92.2 7.6 %copy-start.20 = (bf16[768,8]{0,1:T(8,128)(2,1)}, bf16[768,8]{0,1:T(8,128)(2,1)S(1)}, u32[]{:S(2)}) copy-start(bf16[768,8]{0,1:T(8,128)(2,1)S(1)} %reshape.199) | copy-start | bytes 36868
  94.1 5.7 %copy-start.14 = (bf16[1024,8]{0,1:T(8,128)(2,1)}, bf16[1024,8]{0,1:T(8,128)(2,1)S(1)}, u32[]{:S(2)}) copy-start(bf16[1024,8]{0,1:T(8,128)(2,1)S(1)} %convolution_convert_fusion.3) | copy-start | bytes 49156
  96.1 30.4 %copy-start.16 = (bf16[1024,8]{0,1:T(8,128)(2,1)}, bf16[1024,8]{0,1:T(8,128)(2,1)S(1)}, u32[]{:S(2)}) copy-start(bf16[1024,8]{0,1:T(8,128)(2,1)S(1)} %convolution_convert_fusion.2) | copy-start | bytes 49156
  241.0 59.9 %copy-start.39 = (f32[768]{0:T(1024)S(1)}, f32[768]{0:T(1024)}, u32[]{:S(2)}) copy-start(f32[768]{0:T(1024)} %param.34) | copy-start | bytes 9220
  241.0 59.9 %copy-start.40 = (f32[768]{0:T(1024)S(1)}, f32[768]{0:T(1024)}, u32[]{:S(2)}) copy-start(f32[768]{0:T(1024)} %param.33) | copy-start | bytes 9220
  241.0 168.9 %copy-start.27 = (f32[1024]{0:T(1024)}, f32[1024]{0:T(1024)S(1)}, u32[]{:S(2)}) copy-start(f32[1024]{0:T(1024)S(1)} %broadcast_multiply_fusion.4) | copy-start | bytes 12292
  243.4 166.5 %copy-start.29 = (f32[1024]{0:T(1024)}, f32[1024]{0:T(1024)S(1)}, u32[]{:S(2)}) copy-start(f32[1024]{0:T(1024)S(1)} %add_rsqrt_fusion.1) | copy-start | bytes 12292
  409.8 6.1 %copy-start.32 = (f32[1024]{0:T(1024)}, f32[1024]{0:T(1024)S(1)}, u32[]{:S(2)}) copy-start(f32[1024]{0:T(1024)S(1)} %get-tuple-element.203) | copy-start | bytes 12292
  409.8 6.1 %copy-start.34 = (f32[1024]{0:T(1024)}, f32[1024]{0:T(1024)S(1)}, u32[]{:S(2)}) copy-start(f32[1024]{0:T(1024)S(1)} %get-tuple-element.204) | copy-start | bytes 12292
  438.2 6.8 %copy-start.9 = (bf16[2,512,12,64]{1,3,2,0:T(8,128)(2,1)S(1)}, bf16[2,512,12,64]{1,3,2,0:T(8,128)(2,1)}, u32[]{:S(2)}) copy-start(bf16[2,512,12,64]{1,3,2,0:T(8,128)(2,1)} %get-tuple-element.354) | copy-start | bytes 4718596 | tf_op jit(solution)/shard_map/while
  462.2 6.8 %copy-start.9 = (bf16[2,512,12,64]{1,3,2,0:T(8,128)(2,1)S(1)}, bf16[2,512,12,64]{1,3,2,0:T(8,128)(2,1)}, u32[]{:S(2)}) copy-start(bf16[2,512,12,64]{1,3,2,0:T(8,128)(2,1)} %get-tuple-element.354) | copy-start | bytes 4718596 | tf_op jit(solution)/shard_map/while
  477.6 3.5 copy-start.17
  531.3 4.5 copy-start.37
  (30 other events, 67.0 us)
Sparse Core Ops, SparseCore 0:
  11.0 56.7 all-gather.8
  70.7 53.0 all-gather.10
  126.7 53.0 all-gather.12
  182.5 53.0 all-gather.14
  238.3 62.5 all-gather.16
  303.6 62.4 all-gather.18
where the time goes:
time: 566 us; the launch traced here: 558 us
  matrix products  173 us (31%)
  waiting for transfers between devices  170 us (30%)
  blocking collectives  122 us (22%)
  local copies, waits for them, and re-layouts  51.2 us (9%)
  other arithmetic  27 us (5%)
  between operations  15 us (3%)
    all_gather x1, waiting for transfers between devices, body(): lax.all_gather(w_inner, ('dp', 'fsdp'), axis=0, tiled=True)  57.5 us
    all_gather x1, waiting for transfers between devices, body(): lax.all_gather(w_key, ('dp', 'fsdp'), axis=0, tiled=True)  45.7 us
    all_gather x1, blocking collectives, body(): lax.all_gather(down_value, ('dp', 'fsdp'), axis=0, tiled=True)  43.6 us
    psum x1, blocking collectives, body(): total_q, total_v = lax.psum((local_q, local_v), ('dp', 'fsdp'))  40.9 us
    all_gather x1, blocking collectives, body(): lax.all_gather(down_query, ('dp', 'fsdp'), axis=0, tiled=True)  37.1 us
    dot_general x1, matrix products, body(): inner = jnp.dot(hidden_low, win, preferred_element_type=jnp.float32)  36.5 us
    all_gather x1, waiting for transfers between devices, body(): lax.all_gather(w_outer, ('dp', 'fsdp'), axis=0, tiled=True)  28.7 us
    dot_general x1, matrix products, body(): jnp.dot(grad_inner, win.T, preferred_element_type=jnp.float32)  22.7 us
  transfers between devices with their start and end apart: 6, of which 5 were waited for; matrix products, arithmetic and copies ran while one was open for 19% of the time, Pallas kernels for 0%

commit v1 on v0

v1 whole, which is shorter than its diff:
```python
import functools

import jax
import jax.numpy as jnp
from jax import lax
from jax.experimental import pallas as pl
from jax.experimental.pallas import tpu as pltpu
from jax.sharding import PartitionSpec as P

MESH = pl.DeviceIdType.MESH
D, H, HD, FF, R, SEQ = 768, 12, 64, 3072, 8, 512
HALF = SEQ // 2
PAIRS = H // 2
BF, F32 = jnp.bfloat16, jnp.float32
AXES = ("dp", "fsdp")


def dot(a, b):
    return lax.dot_general(a, b, (((1,), (0,)), ((), ())), preferred_element_type=F32)


def dot_nt(a, b):
    return lax.dot_general(a, b, (((1,), (1,)), ((), ())), preferred_element_type=F32)


def dot_tn(a, b):
    return lax.dot_general(a, b, (((0,), (0,)), ((), ())), preferred_element_type=F32)


def place():
    dp, fs = lax.axis_index("dp"), lax.axis_index("fsdp")
    return dp // 2, dp % 2, fs // 2, fs % 2


def device(z, x, y, c):
    return (z * 2 + x, y * 2 + c)


def gather_kernel(groups, *refs):
    xs, outs = refs[:groups], refs[groups : 2 * groups]
    ssem, rsem, lsem = refs[2 * groups :]
    z, x, y, c = place()

    def column(x, y, c):
        return (x * 2 + y) * 2 + c

    xa, ya = jnp.where(c == 0, x, 1 - x), jnp.where(c == 0, 1 - y, y)
    xb, yb = jnp.where(c == 0, 1 - x, x), jnp.where(c == 0, y, 1 - y)
    near, far, twin = device(z, xa, ya, c), device(z, xb, yb, c), device(z, x, y, 1 - c)
    line = [device((z + d) % 4, x, y, c) for d in (1, 2, 3)]
    barrier = pltpu.get_barrier_semaphore()
    for other in (*line, near, far, twin):
        pl.semaphore_signal(barrier, 1, device_id=other, device_id_type=MESH)
    pl.semaphore_wait(barrier, 6)
    mine, at_near, at_far, at_diag = column(x, y, c), column(xa, ya, c), column(xb, yb, c), column(1 - x, 1 - y, c)

    def remote(g, src, dst, k, to):
        pltpu.make_async_remote_copy(
            src_ref=src, dst_ref=dst, send_sem=ssem.at[g], recv_sem=rsem.at[g, k], device_id=to, device_id_type=MESH
        ).start()

    def wait(ref, sem):
        pltpu.make_async_copy(ref, ref, sem).wait()

    def pass_on(g, col, k, to):
        remote(g, outs[g].at[:, col], outs[g].at[:, col], k, to)

    def own(g):
        pltpu.make_async_copy(xs[g], outs[g].at[z, mine], lsem.at[g]).start()
        for d in range(3):
            remote(g, xs[g], outs[g].at[z, mine], d, line[d])

    def after_line(g):
        pltpu.make_async_copy(xs[g], outs[g].at[z, mine], lsem.at[g]).wait()
        for d in range(3):
            wait(xs[g], rsem.at[g, d])
        pass_on(g, mine, 3, near)
        pass_on(g, mine, 4, far)
        pass_on(g, mine, 6, twin)

    def after_near(g):
        wait(outs[g].at[:, at_near], rsem.at[g, 3])
        pass_on(g, at_near, 5, far)
        pass_on(g, at_near, 7, twin)

    def after_far(g):
        wait(outs[g].at[:, at_far], rsem.at[g, 4])
        pass_on(g, at_far, 8, twin)

    def after_diag(g):
        wait(outs[g].at[:, at_diag], rsem.at[g, 5])
        pass_on(g, at_diag, 9, twin)

    stages = (own, after_line, after_near, after_far, after_diag)
    for t in range(groups + len(stages)):
        for k, stage in enumerate(stages):
            if 0 <= t - k < groups:
                stage(t - k)
    for g in range(groups):
        for k in range(4):
            wait(outs[g].at[:, mine], rsem.at[g, 6 + k])
        for _ in range(3):
            wait(xs[g], ssem.at[g])
        for _ in range(7):
            wait(outs[g].at[:, mine], ssem.at[g])


def gather_all(mesh, blocks):
    n = mesh.size
    if dict(mesh.shape) != {"dp": 8, "fsdp": 4} or any(b.shape[0] % 8 for b in blocks):
        return [lax.all_gather(b, AXES, axis=0, tiled=True) for b in blocks]
    k = len(blocks)
    got = pl.pallas_call(
        functools.partial(gather_kernel, k),
        out_shape=[jax.ShapeDtypeStruct((4, 8, *b.shape), b.dtype) for b in blocks],
        in_specs=[pl.BlockSpec(memory_space=pl.ANY)] * k,
        out_specs=[pl.BlockSpec(memory_space=pl.ANY)] * k,
        scratch_shapes=[
            pltpu.SemaphoreType.DMA((k,)),
            pltpu.SemaphoreType.DMA((k, 10)),
            pltpu.SemaphoreType.DMA((k,)),
        ],
        compiler_params=pltpu.CompilerParams(collective_id=0, has_side_effects=True),
        name="gather_weights",
    )(*blocks)
    return [g.reshape(n * b.shape[0], b.shape[1]) for g, b in zip(got, blocks)]


def reduce_kernel(q_ref, v_ref, oq_ref, ov_ref, pair, plane, line, ssem, rsem):
    z, x, y, c = place()
    twin = device(z, x, y, 1 - c)
    chips = [(x, 1 - y), (1 - x, y), (1 - x, 1 - y)]
    planes = [(z + d) % 4 for d in (1, 2, 3)]
    barrier = pltpu.get_barrier_semaphore()
    others = [twin] + [device(z, i, j, c) for i, j in chips] + [device(k, x, y, c) for k in planes]
    for other in others:
        pl.semaphore_signal(barrier, 1, device_id=other, device_id_type=MESH)
    pl.semaphore_wait(barrier, 7)

    def copy(src, dst, k, to):
        return pltpu.make_async_remote_copy(
            src_ref=src, dst_ref=dst, send_sem=ssem.at[k], recv_sem=rsem.at[k], device_id=to, device_id_type=MESH
        )

    first = c == 0
    pair[0] = jnp.where(first, v_ref[...], q_ref[...])
    swap = copy(pair.at[0], pair.at[1], 0, twin)
    swap.start()
    swap.wait()
    plane[x * 2 + y] = jnp.where(first, q_ref[...], v_ref[...]) + pair[1]
    sends = [copy(plane.at[x * 2 + y], plane.at[x * 2 + y], 1 + k, device(z, i, j, c)) for k, (i, j) in enumerate(chips)]
    for s in sends:
        s.start()
    for s in sends:
        s.wait()
    line[z] = (plane[0] + plane[1]) + (plane[2] + plane[3])
    sends = [copy(line.at[z], line.at[z], 4 + k, device(to, x, y, c)) for k, to in enumerate(planes)]
    for s in sends:
        s.start()
    for s in sends:
        s.wait()
    pair[2] = (line[0] + line[1]) + (line[2] + line[3])
    swap = copy(pair.at[2], pair.at[3], 7, twin)
    swap.start()
    swap.wait()
    oq_ref[...] = jnp.where(first, pair[2], pair[3])
    ov_ref[...] = jnp.where(first, pair[3], pair[2])


def sum_all(mesh, q, v):
    if dict(mesh.shape) != {"dp": 8, "fsdp": 4}:
        return lax.psum((q, v), AXES)
    shape = jax.ShapeDtypeStruct(q.shape, F32)
    vmem = pl.BlockSpec(memory_space=pltpu.VMEM)
    return pl.pallas_call(
        reduce_kernel,
        out_shape=[shape, shape],
        in_specs=[vmem, vmem],
        out_specs=[vmem, vmem],
        scratch_shapes=[pltpu.VMEM((4, *q.shape), F32)] * 3
        + [pltpu.SemaphoreType.DMA((8,)), pltpu.SemaphoreType.DMA((8,))],
        compiler_params=pltpu.CompilerParams(collective_id=1, has_side_effects=True),
        name="sum_grads",
    )(q, v)


def gelu_parts(u):
    dens = jnp.exp(u * u * -0.5)
    t = 1.0 / (jnp.abs(u) * (0.3275911 * 0.7071067811865476) + 1.0)
    poly = ((((1.061405429 * t - 1.453152027) * t + 1.421413741) * t - 0.284496736) * t + 0.254829592) * t
    tail = poly * dens * 0.5
    phi = jnp.where(u < 0, tail, 1.0 - tail)
    return u * phi, phi + u * dens * 0.3989422804014327


def layer_kernel(
    seg_ref, x_ref, g_ref, wq, wk, wv, wo, win, wout, down, up_q, up_v, g1, b1, g2, b2,
    y_ref, tg_ref, gq_ref, gv_ref,
    perm_s, permt_s, bias_s, xr_s, low_s, qkv_s, p_s, ctx_s, n1_s, r1_s, hb_s, act_s, gp_s, dz_s, db_s, dqkv_s,
):
    row = pl.program_id(0)
    seg = jnp.broadcast_to(seg_ref[pl.ds(row, 1), :], (8, SEQ))
    lane = lax.broadcasted_iota(jnp.int32, (8, SEQ), 1)
    hit = (seg == pltpu.roll(seg, SEQ - HALF + 1, 1)) & (lane <= HALF)
    a = jnp.min(jnp.where(hit, lane, SEQ), axis=1, keepdims=True)[0:1]
    i = lax.broadcasted_iota(jnp.int32, (SEQ, SEQ), 0)
    j = lax.broadcasted_iota(jnp.int32, (SEQ, SEQ), 1)
    diff = j - i
    perm_s[...] = jnp.where((diff == a) | (diff == a - SEQ), 1.0, 0.0).astype(BF)
    permt_s[...] = jnp.where((diff == -a) | (diff == SEQ - a), 1.0, 0.0).astype(BF)
    segb = seg.astype(F32).astype(BF)
    seg_row = dot_nt(segb, perm_s[HALF:, :])[0:1]
    seg_col = dot_nt(perm_s[HALF:, :], segb)[:, 0:1]
    bias = jnp.where(seg_col == seg_row, 0.0, -1e30)
    bias_s[:, :HALF] = bias
    bias_s[:, HALF:] = bias

    xr_s[...] = dot(perm_s[...], x_ref[0]).astype(BF)
    low_s[...] = dot(xr_s[...], down[...]).astype(BF)

    for n in range(3):
        cols = slice(256 * n, 256 * n + 256)
        q = dot(xr_s[...], wq[:, cols]) + 2.0 * dot(low_s[:, :R], up_q[:, cols])
        v = dot(xr_s[...], wv[:, cols]) + 2.0 * dot(low_s[:, R:], up_v[:, cols])
        qkv_s[:, 256 * n : 256 * n + 256] = q.astype(BF)
        qkv_s[:, D + 256 * n : D + 256 * n + 256] = dot(xr_s[...], wk[:, cols]).astype(BF)
        qkv_s[:, 2 * D + 256 * n : 2 * D + 256 * n + 256] = v.astype(BF)

    low_half = lax.broadcasted_iota(jnp.int32, (HALF, 2 * HD), 1) < HD
    top_half = lax.broadcasted_iota(jnp.int32, (2 * HD, HALF), 0) < HD
    zero = jnp.zeros((HALF, 2 * HD), BF)

    def two(v):
        return jnp.concatenate([jnp.where(low_half, v, zero), jnp.where(low_half, zero, v)], axis=0)

    def pick(v):
        return jnp.where(top_half, v[:, :HALF], v[:, HALF:])

    def heads(p, carry):
        for b in range(2):
            rows = slice(HALF * b, HALF * (b + 1))
            cut = [pl.ds(pl.multiple_of(D * w + 2 * HD * p, 128), 2 * HD) for w in range(3)]
            q, k, v = (qkv_s[rows, c] for c in cut)
            s = dot_nt(k, two(q * 0.125))
            if b == 1:
                s = s + bias_s[...]
            e = jnp.exp(s - jnp.max(s, axis=0, keepdims=True))
            pr = (e * (1.0 / jnp.sum(e, axis=0, keepdims=True))).astype(BF)
            p_s[p, b] = pr
            ctx_s[rows, cut[0]] = pick(dot_tn(v, pr)).T.astype(BF)
        return carry

    lax.fori_loop(0, PAIRS, heads, 0)

    z1 = xr_s[...].astype(F32) + dot(ctx_s[...], wo[...])
    z1 = z1 - jnp.mean(z1, axis=-1, keepdims=True)
    r1 = lax.rsqrt(jnp.mean(z1 * z1, axis=-1, keepdims=True) + 1e-5)
    n1 = z1 * r1
    n1_s[...] = n1
    r1_s[...] = r1
    hb_s[...] = (n1 * g1[...][None] + b1[...][None]).astype(BF)

    def inner(n, carry):
        cols = pl.ds(pl.multiple_of(512 * n, 512), 512)
        act, slope = gelu_parts(dot(hb_s[...], win[:, cols]))
        act_s[:, cols] = act.astype(BF)
        gp_s[:, cols] = slope
        return carry

    lax.fori_loop(0, FF // 512, inner, 0)

    z2 = n1_s[...] * g1[...][None] + b1[...][None] + dot(act_s[...], wout[...])
    z2 = z2 - jnp.mean(z2, axis=-1, keepdims=True)
    r2 = lax.rsqrt(jnp.mean(z2 * z2, axis=-1, keepdims=True) + 1e-5)
    n2 = z2 * r2
    y_ref[0] = dot(permt_s[...], (n2 * g2[...][None] + b2[...][None]).astype(BF)).astype(BF)
    dn2 = dot(perm_s[...], g_ref[0]) * g2[...][None]
    dz2 = r2 * (dn2 - jnp.mean(dn2, axis=-1, keepdims=True) - n2 * jnp.mean(dn2 * n2, axis=-1, keepdims=True))
    dz_s[...] = dz2
    db_s[...] = dz2.astype(BF)

    def inner_back(n, carry):
        cols = pl.ds(pl.multiple_of(512 * n, 512), 512)
        act_s[:, cols] = (dot_nt(db_s[...], wout[cols, :]) * gp_s[:, cols]).astype(BF)
        return carry

    lax.fori_loop(0, FF // 512, inner_back, 0)

    dn1 = (dz_s[...] + dot_nt(act_s[...], win[...])) * g1[...][None]
    n1 = n1_s[...]
    dz1 = r1_s[...] * (dn1 - jnp.mean(dn1, axis=-1, keepdims=True) - n1 * jnp.mean(dn1 * n1, axis=-1, keepdims=True))
    dz_s[...] = dz1
    ctx_s[...] = dot_nt(dz1.astype(BF), wo[...]).astype(BF)

    def heads_back(p, carry):
        for b in range(2):
            rows = slice(HALF * b, HALF * (b + 1))
            cut = [pl.ds(pl.multiple_of(D * w + 2 * HD * p, 128), 2 * HD) for w in range(3)]
            q, k, v = (qkv_s[rows, c] for c in cut)
            dc = two(ctx_s[rows, cut[0]])
            pr = p_s[p, b]
            dqkv_s[rows, cut[2]] = dot(pr, dc).astype(BF)
            dp = dot_nt(v, dc)
            prf = pr.astype(F32)
            ds = (prf * (dp - jnp.sum(prf * dp, axis=0, keepdims=True))).astype(BF)
            dqkv_s[rows, cut[1]] = dot(ds, two(q * 0.125)).astype(BF)
            dqkv_s[rows, cut[0]] = (pick(dot_tn(k, ds)).T * 0.125).astype(BF)
        return carry

    lax.fori_loop(0, PAIRS, heads_back, 0)

    dq, dv = dqkv_s[:, :D], dqkv_s[:, 2 * D :]
    gq = 2.0 * dot_tn(low_s[:, :R], dq)
    gv = 2.0 * dot_tn(low_s[:, R:], dv)
    gq_ref[...] = jnp.where(row == 0, gq, gq_ref[...] + gq)
    gv_ref[...] = jnp.where(row == 0, gv, gv_ref[...] + gv)
    dlow_q = (2.0 * dot_nt(dq, up_q[...])).astype(BF)
    dlow_v = (2.0 * dot_nt(dv, up_v[...])).astype(BF)
    tg = dz_s[...] + dot_nt(dq, wq[...]) + dot_nt(dqkv_s[:, D : 2 * D], wk[...]) + dot_nt(dv, wv[...])
    tg = tg + dot_nt(dlow_q, down[:, :R]) + dot_nt(dlow_v, down[:, R:])
    tg_ref[0] = dot(permt_s[...], tg.astype(BF)).astype(BF)


def run_layer(seg, x, g, wq, wk, wv, wo, win, wout, down, up_q, up_v, g1, b1, g2, b2):
    rows = x.shape[0]

    def whole(v):
        return pl.BlockSpec(v.shape, lambda r: (0,) * v.ndim, pipeline_mode=pl.Buffered(1))

    per_row = pl.BlockSpec((1, SEQ, D), lambda r: (r, 0, 0))
    consts = (wq, wk, wv, wo, win, wout, down, up_q, up_v, g1, b1, g2, b2)
    grad = jax.ShapeDtypeStruct((R, D), F32)
    act = jax.ShapeDtypeStruct(x.shape, BF)
    return pl.pallas_call(
        layer_kernel,
        grid=(rows,),
        out_shape=[act, act, grad, grad],
        in_specs=[whole(seg), per_row, per_row, *map(whole, consts)],
        out_specs=[per_row, per_row] + [pl.BlockSpec((R, D), lambda r: (0, 0))] * 2,
        scratch_shapes=[
            pltpu.VMEM((SEQ, SEQ), BF),
            pltpu.VMEM((SEQ, SEQ), BF),
            pltpu.VMEM((HALF, SEQ), F32),
            pltpu.VMEM((SEQ, D), BF),
            pltpu.VMEM((SEQ, 2 * R), BF),
            pltpu.VMEM((SEQ, 3 * D), BF),
            pltpu.VMEM((PAIRS, 2, HALF, SEQ), BF),
            pltpu.VMEM((SEQ, D), BF),
            pltpu.VMEM((SEQ, D), F32),
            pltpu.VMEM((SEQ, 1), F32),
            pltpu.VMEM((SEQ, D), BF),
            pltpu.VMEM((SEQ, FF), BF),
            pltpu.VMEM((SEQ, FF), F32),
            pltpu.VMEM((SEQ, D), F32),
            pltpu.VMEM((SEQ, D), BF),
            pltpu.VMEM((SEQ, 3 * D), BF),
        ],
        compiler_params=pltpu.CompilerParams(vmem_limit_bytes=60 << 20),
        name="layer_rows",
    )(seg, x, g, *consts)


def solution(mesh):
    def body(
        tokens, segments, w_query, w_key, w_value, w_output, w_inner, w_outer, down_query, down_value,
        up_query, up_value, norm1_gain, norm1_shift, norm2_gain, norm2_shift, out_grad,
    ):
        down = jnp.concatenate([down_query, down_value], axis=1)
        mats = gather_all(mesh, [down, w_query, w_key, w_value, w_output, w_inner, w_outer])
        norms = (norm1_gain, norm1_shift, norm2_gain, norm2_shift)
        y, tg, gq, gv = run_layer(segments, tokens, out_grad, *mats[1:], mats[0], up_query, up_value, *norms)
        gq, gv = sum_all(mesh, gq, gv)
        return y, tg, gq, gv

    split, copied = P(AXES), P()
    return jax.shard_map(
        body,
        mesh=mesh,
        in_specs=(split,) * 10 + (copied,) * 6 + (split,),
        out_specs=(split, split, copied, copied),
        check_vma=False,
    )
```

time: 566 us -> 193 us (0.34); the launches traced: 558 us -> 193 us
  Pallas kernels: 0 us -> 187 us
  matrix products: 173 us -> 0 us
  waiting for transfers between devices: 170 us -> 0 us
  blocking collectives: 122 us -> 0 us
  local copies, waits for them, and re-layouts: 51.2 us -> 4.22 us
  other arithmetic: 27 us -> 0.67 us
  between operations: 15 us -> 0.65 us
    pallas_call x0 -> x3, Pallas kernels: none -> 187 us  [the longest x1 94 us: run_layer(): pl.pallas_call(layer_kernel, grid=(rows,), out_shape=[act, act, grad, gra...]
    dot_general x33 -> x0, matrix products: 173 us -> none  [the longest x1 36.5 us: body(): inner = jnp.dot(hidden_low, win, preferred_element_type=jnp.float32)]
    all_gather x6 -> x0, waiting for transfers between devices: 167 us -> none  [the longest x1 57.5 us: body(): lax.all_gather(w_inner, ('dp', 'fsdp'), axis=0, tiled=True)]
    all_gather x2 -> x0, blocking collectives: 80.7 us -> none  [the longest x1 43.6 us: body(): lax.all_gather(down_value, ('dp', 'fsdp'), axis=0, tiled=True)]
    psum x1 -> x0, blocking collectives: 40.9 us -> none  [body(): total_q, total_v = lax.psum((local_q, local_v), ('dp', 'fsdp'))]
    while x36 -> x0, local copies, waits for them, and re-layouts: 20.9 us -> none  [the longest x4 9.35 us: body(): lax.map(attend, (q_heads, k_heads, v_heads, segments))]
    convert_element_type x2 -> x0, other arithmetic: 13.7 us -> none  [attend_back(): grad_scores = (probs * (grad_probs - inner_sum)).astype(jnp.bfloat16)]
    reshape x4 -> x0, local copies, waits for them, and re-layouts: 10.9 us -> none  [the longest x1 3.84 us: body(): grad_heads = grad_context.reshape(row_count, length, H, HD)]
  transfers between devices with their start and end apart: 6 -> 0, of which waited for: 5 -> 0; matrix products, arithmetic and copies ran while one was open for 19% -> 0% of each run, Pallas kernels for 0% -> 0%
where the time goes in v1:
time: 193 us
  Pallas kernels  187 us (97%)
  local copies, waits for them, and re-layouts  4.22 us (2%)
    pallas_call x1, Pallas kernels, run_layer(): pl.pallas_call(layer_kernel, grid=(rows,), out_shape=[act, act, grad, gra...  94 us
    pallas_call x1, Pallas kernels, gather_all(): pl.pallas_call(functools.partial(gather_kernel, k), out_shape=[jax.ShapeD...  73.2 us
    pallas_call x1, Pallas kernels, sum_all(): pl.pallas_call(reduce_kernel, out_shape=[shape, shape], in_specs=[vmem, v...  19.8 us
    unnamed x4, local copies, waits for them, and re-layouts  4.22 us

profile of v1, /device:TPU:0, one launch (start us, length us, event | category | flops | bytes accessed | tf_op | source)
XLA Modules:
  0.0 192.6 jit_solution(3473564466461455114)
XLA Ops:
  0.6 0.8 copy.21
  1.4 0.8 copy.22
  2.2 0.7 pad_maximum_fusion.refs_0_
  2.8 73.2 %gather_weights.1 = (bf16[4,8,24,16]{3,2,1,0:T(8,128)(2,1)}, bf16[4,8,24,768]{3,2,1,0:T(8,128)(2,1)}, bf16[4,8,24,768]{3,2,1,0:T(8,128)(2,1)}, bf16[4,8,24,768]{...) custom-call(bf16[24,16]{1,0:T(8,128)(2,1)} %pad_maximum_fusion.refs_, ...), custom_call_target="tpu_custom_call" | custom-call | tf_op jit(solution)/shard_map/gather_weights/pallas_call | solution.py:113
  76.0 94.0 %layer_rows.1 = (bf16[2,512,768]{2,1,0:T(8,128)(2,1)}, bf16[2,512,768]{2,1,0:T(8,128)(2,1)}, f32[8,768]{1,0:T(8,128)}, f32[8,768]{1,0:T(8,128)}) custom-call(s32[2,512]{1,0:T(2,128)} %seg_ref.1, bf16[2,512,768]{2,1,0:T(8,128)(2,1)} %x_ref.1, bf16[2,512,768]{2,1,0:T(8,128)(2,1)} %g_ref.1, bf16[768,768]{1,0:T(8,128)(2,1)} %bitcast.9, ...), custom_call_target="tpu_custom_call" | custom-call | tf_op jit(solution)/shard_map/layer_rows/pallas_call | solution.py:334
  170.1 19.8 %sum_grads.1 = (f32[8,768]{1,0:T(8,128)}, f32[8,768]{1,0:T(8,128)}) custom-call(f32[8,768]{1,0:T(8,128)} %get-tuple-element.26.q_ref, f32[8,768]{1,0:T(8,128)} %get-tuple-element.27.v_ref), custom_call_target="tpu_custom_call" | custom-call | tf_op jit(solution)/shard_map/sum_grads/pallas_call | solution.py:175
  189.9 1.3 copy.25
  191.3 1.3 copy.26
